TPU v7x, 256 devices: a whole 4x4x8 slice. The times are simulated.
256 devices in a mesh: row: 16 (over z, core), col: 4 (over x), inner: 4 (over y).
Axes of the slice: x: 4, y: 4, z: 8, core: 2. Of those that a mesh axis runs over, the one named last changes fastest.
Arguments:
- density: bfloat16 [64, 16, 256, 256], P('row', ('col', 'inner')), may hold values from -1.5 to 1.5, as said below
- block_cols: int32 [64, 16], replicated, may hold values from 0 to 63, as said below
- mixing: float32 [3], replicated, may hold values from 0.02 to 1.5, as said below
Outputs:
- purified: bfloat16 [64, 16, 256, 256], P('row', ('col', 'inner'))
Inputs may be any that keep to these rules, and one draw needn't show every extreme that they name: Slot g of block row i names a block row of group g (rows g * 4 to g * 4 + 3); within one group of block rows, slot g names each row of group g once. Slot i // 4 of row i names i itself. The pattern is symmetric: row block_cols[i, g] names i in slot i // 4. It is consistent: block_cols[block_cols[i, t], g] == block_cols[i, g] for all i, t, g. `density`: block (i, g) is the transpose of block (block_cols[i, g], i // 4). `mixing`: element 0 lies in 0.5 to 1.5, elements 1 and 2 in 0.02 to 0.05.
All inputs are finite; a program needn't handle non-finite values.
Results may differ from a plain program's by a relative error of at most 0.007.
Values may be sent and summed in bfloat16 or wider, within the bound.
No kernel may reach another device: no remote copies, remote signals or barrier semaphores. Data moves between devices by JAX's collectives and lax.ppermute only.
A program may use at most 128 MiB of HBM per device.

v0:
```python
import jax
import jax.numpy as jnp
from jax import lax
from jax.sharding import PartitionSpec as P

GS = 4


def laid_out(tiles, dim):
    tiles = jnp.moveaxis(tiles, 0, dim)
    shape = tiles.shape
    return tiles.reshape(*shape[:dim], shape[dim] * shape[dim + 1], *shape[dim + 2 :])


def from_everyone(shard, axis):
    size = lax.axis_size(axis)
    return lax.all_to_all(
        jnp.broadcast_to(shard[None], (size, *shard.shape)), axis, 0, 0, tiled=True
    )


def gathered_copies(shard, axis, dim):
    return laid_out(from_everyone(shard, axis), dim)


def fold_with(panel, piece):
    return jnp.einsum("htab,tgbc->hgac", panel, piece, preferred_element_type=jnp.float32)


def clique_filter(density, block_cols, mixing, row_start):
    row_count = density.shape[0]
    width = density.shape[2]
    groups_here = row_count // GS
    first_group = row_start // GS
    leaders = lax.dynamic_slice_in_dim(block_cols[:GS], first_group, groups_here, 1)
    ordered = density[:, 0][(leaders - row_start).reshape(-1)]
    ordered = ordered.reshape(GS, groups_here, 1, width, width)
    arrived = lax.all_to_all(ordered, "inner", split_axis=0, concat_axis=2, tiled=True)
    blocks = arrived[0]
    slot_count = blocks.shape[1]
    slot_start = lax.axis_index("col") * slot_count
    density_panel = gathered_copies(blocks, "col", 1)
    square = fold_with(density_panel, lax.all_gather(blocks, "row", axis=0, tiled=True)).astype(
        jnp.bfloat16
    )
    group_ids = first_group + jnp.arange(groups_here, dtype=jnp.int32)
    slot_ids = slot_start + jnp.arange(slot_count, dtype=jnp.int32)
    on_diagonal = (group_ids[:, None] == slot_ids[None, :]).astype(jnp.float32)
    identity = jnp.eye(width, dtype=jnp.float32)
    mixer_blocks = (
        mixing[0] * on_diagonal[:, :, None, None] * identity
        + mixing[1] * blocks.astype(jnp.float32)
        + mixing[2] * square.astype(jnp.float32)
    ).astype(jnp.bfloat16)
    square_panel = gathered_copies(square, "col", 1)
    filtered = fold_with(
        square_panel, lax.all_gather(mixer_blocks, "row", axis=0, tiled=True)
    ).astype(jnp.bfloat16)
    returned = lax.all_to_all(filtered[None], "inner", split_axis=2, concat_axis=0, tiled=True)
    regrouped = returned.reshape(GS * groups_here, 1, width, width)
    local_rows = row_start + jnp.arange(row_count, dtype=jnp.int32)
    clique_ids = lax.dynamic_slice_in_dim(block_cols[:, 0], row_start, row_count, 0)
    positions = clique_ids * groups_here + (local_rows // GS - first_group)
    return regrouped[positions]


def body(density, block_cols, mixing):
    row_count = density.shape[0]
    row_start = lax.axis_index("row") * row_count
    return clique_filter(density, block_cols, mixing, row_start)


def solution(mesh):
    in_specs = (P("row", ("col", "inner"), None, None), P(), P())
    out_specs = P("row", ("col", "inner"), None, None)
    return jax.shard_map(body, mesh=mesh, in_specs=in_specs, out_specs=out_specs, check_vma=False)
```

profile of v0, /device:TPU:1, one launch (start us, length us, event | category | flops | bytes accessed | tf_op | source)
XLA Modules:
  0.0 174.0 jit_solution(14277715915551514343)
XLA Ops:
  6.5 0.0 copy-start
  6.5 0.0 all-gather.6.cloned.1.call-start
  6.5 0.8 fusion.6
  7.3 0.3 copy-done
  7.6 0.6 gather_fusion
  8.2 0.2 copy.15
  8.4 13.4 %all_to_all.28 = bf16[4,1,1,256,256]{3,4,2,1,0:T(8,128)(2,1)S(1)} all-to-all(bf16[4,1,1,256,256]{3,4,2,1,0:T(8,128)(2,1)S(1)} %copy.15), channel_id=1, replica_groups=mesh['row'=16,'col'=4,'inner'=4] {'inner'}, dimensions={0} | all-to-all | bytes 1048576 | tf_op jit(solution)/shard_map/all_to_all | solution.py:38
  21.8 1.0 copy.17
  22.8 0.0 all-gather.6.cloned.1.call-update
  22.8 0.2 copy.18
  23.0 1.6 broadcast_in_dim.11
  24.6 0.0 copy-start.1
  24.6 4.1 %all-to-all-start.1 = ((bf16[4,1,4,256,256]{4,3,2,1,0:T(8,128)(2,1)}), bf16[4,1,4,256,256]{4,3,2,1,0:T(8,128)(2,1)S(1)}, u32[]{:S(2)}, u32[]{:S(2)}) async-start(bf16[4,1,4,256,256]{4,3,2,1,0:T(8,128)(2,1)} %broadcast_in_dim.11), calls=%async_computation.1 | async-start | bytes 4194304 | tf_op jit(solution)/shard_map/all_to_all | solution.py:17
  28.8 0.0 all-gather.4.cloned.1.call-start
  28.8 0.0 copy-done.1
  28.8 0.6 fusion.8
  29.4 0.6 compare_select_fusion.2
  30.0 23.1 %all-to-all-done.1 = bf16[4,1,4,256,256]{4,3,2,1,0:T(8,128)(2,1)S(1)} async-done(((bf16[4,1,4,256,256]{4,3,2,1,0:T(8,128)(2,1)}), bf16[4,1,4,256,256]{4,3,2,1,0:T(8,128)(2,1)S(1)}, u32[]{:S(2)}, u32[]{:S(2)}) %all-to-all-start.1) | async-done | bytes 2097184 | tf_op jit(solution)/shard_map/all_to_all | solution.py:17
  53.1 28.2 %all-gather.6.cloned.1.call-done = bf16[64,1,1,256,256]{4,3,2,1,0:T(8,128)(2,1)} async-done(((bf16[4,1,1,256,256]{4,3,2,1,0:T(8,128)(2,1)}), bf16[64,1,1,256,256]{4,3,2,1,0:T(8,128)(2,1)}) %all-gather.6.cloned.1.call-update) | async-done | bytes 8388624 | tf_op jit(solution)/shard_map/all_gather | solution.py:43
  81.3 8.0 %fusion.4 = (bf16[1,4,256,256]{2,3,1,0:T(8,128)(2,1)}, bf16[4,256,256]{2,1,0:T(8,128)(2,1)}) fusion(bf16[4,1,1,256,256]{3,4,2,1,0:T(8,128)(2,1)S(1)} %all_to_all.28, f32[]{:T(128)} %bitcast.1, f32[]{:T(128)} %bitcast.7, f32[256,256]{0,1:T(8,128)S(1)} %fusion.5, f32[4]{0:T(128)S(1)} %compare_select_fusion.2, bf16[16,4,256,256]{3,2,1,0:T(8,128)(2,1)} %bitcast.69, ...), kind=kOutput, calls=%fused_computation.9 | convolution fusion | flops 2149842944 | bytes 12320792 | tf_op jit(solution)/shard_map/htab,tgbc->hgac/dot_general | solution.py:27
  89.3 2.1 %copy.20 = bf16[1,4,256,256]{3,2,1,0:T(8,128)(2,1)} copy(bf16[1,4,256,256]{2,3,1,0:T(8,128)(2,1)} %get-tuple-element.8) | data formatting | bytes 1048576 | tf_op jit(solution)/shard_map/convert_element_type | solution.py:54
  91.4 0.0 all-gather.4.cloned.1.call-update
  91.4 1.2 copy.21
  92.7 0.2 broadcast_in_dim.26
  92.9 29.6 %all_to_all.29 = bf16[4,1,4,256,256]{4,3,2,1,0:T(8,128)(2,1)S(1)} all-to-all(bf16[4,1,4,256,256]{4,3,2,1,0:T(8,128)(2,1)S(1)} %broadcast_in_dim.26), channel_id=1, replica_groups=mesh['row'=16,'col'=4,'inner'=4] {'col'}, dimensions={0} | all-to-all | bytes 4194304 | tf_op jit(solution)/shard_map/all_to_all | solution.py:17
  122.5 23.5 %all-gather.4.cloned.1.call-done = bf16[16,4,256,256]{3,2,1,0:T(8,128)(2,1)} async-done(((bf16[1,4,256,256]{3,2,1,0:T(8,128)(2,1)}), bf16[16,4,256,256]{3,2,1,0:T(8,128)(2,1)}) %all-gather.4.cloned.1.call-update) | async-done | bytes 8388624 | tf_op jit(solution)/shard_map/all_gather | solution.py:57
  146.0 6.5 %fusion.2 = bf16[1,1,4,256,256]{3,4,1,0,2:T(8,128)(2,1)} fusion(bf16[16,4,256,256]{3,2,1,0:T(8,128)(2,1)} %all-gather.4.cloned.1.call-done, bf16[16,256,256,1]{2,1,3,0:T(8,128)(2,1)S(1)} %bitcast.63), kind=kOutput, calls=%fused_computation.6 | convolution fusion | flops 2147745792 | bytes 11010048 | tf_op jit(solution)/shard_map/htab,tgbc->hgac/dot_general | solution.py:27
  152.5 4.0 %all-to-all-start.3 = ((bf16[1,1,4,256,256]{3,4,1,0,2:T(8,128)(2,1)}), bf16[1,1,4,256,256]{3,4,1,0,2:T(8,128)(2,1)S(1)}, u32[]{:S(2)}, u32[]{:S(2)}) async-start(bf16[1,1,4,256,256]{3,4,1,0,2:T(8,128)(2,1)} %fusion.2), calls=%async_computation.3 | async-start | bytes 1048576 | tf_op jit(solution)/shard_map/all_to_all | solution.py:59
  156.5 0.7 slice.19
  157.2 0.1 fusion.7
  157.3 8.2 %all-to-all-done.3 = bf16[1,1,4,256,256]{3,4,1,0,2:T(8,128)(2,1)S(1)} async-done(((bf16[1,1,4,256,256]{3,4,1,0,2:T(8,128)(2,1)}), bf16[1,1,4,256,256]{3,4,1,0,2:T(8,128)(2,1)S(1)}, u32[]{:S(2)}, u32[]{:S(2)}) %all-to-all-start.3) | async-done | bytes 524320 | tf_op jit(solution)/shard_map/all_to_all | solution.py:59
  165.6 0.6 gather_fusion.1
  166.1 1.0 copy.24
  (3 shorter events, 0.0 us)
Async XLA Ops:
  6.5 1.1 copy-start
  6.5 74.8 %all-gather.6.cloned.1.call-start = ((), (), s32[]{:S(2)}) async-start(), calls=%async_computation.5 | async-start | bytes 8912896 | tf_op jit(solution)/shard_map/all_gather | solution.py:43
  24.6 4.2 %copy-start.1 = (f32[3]{0:T(128)S(1)}, f32[3]{0:T(128)}, u32[]{:S(2)}) copy-start(f32[3]{0:T(128)} %param.5) | copy-start | bytes 40
  24.6 28.5 %all-to-all-start.1 = ((bf16[4,1,4,256,256]{4,3,2,1,0:T(8,128)(2,1)}), bf16[4,1,4,256,256]{4,3,2,1,0:T(8,128)(2,1)S(1)}, u32[]{:S(2)}, u32[]{:S(2)}) async-start(bf16[4,1,4,256,256]{4,3,2,1,0:T(8,128)(2,1)} %broadcast_in_dim.11), calls=%async_computation.1 | async-start | bytes 4194304 | tf_op jit(solution)/shard_map/all_to_all | solution.py:17
  28.8 117.2 %all-gather.4.cloned.1.call-start = ((), (), s32[]{:S(2)}) async-start(), calls=%async_computation.4 | async-start | bytes 8912896 | tf_op jit(solution)/shard_map/all_gather | solution.py:57
  152.5 13.0 %all-to-all-start.3 = ((bf16[1,1,4,256,256]{3,4,1,0,2:T(8,128)(2,1)}), bf16[1,1,4,256,256]{3,4,1,0,2:T(8,128)(2,1)S(1)}, u32[]{:S(2)}, u32[]{:S(2)}) async-start(bf16[1,1,4,256,256]{3,4,1,0,2:T(8,128)(2,1)} %fusion.2), calls=%async_computation.3 | async-start | bytes 1048576 | tf_op jit(solution)/shard_map/all_to_all | solution.py:59
Sparse Core Ops, SparseCore 0:
  23.0 58.3 all-gather.5
  91.5 54.3 all-gather.3
where the time goes:
time: 175 us; the launch traced here: 174 us
  waiting for transfers between devices  83 us (47%)
  blocking collectives  43.1 us (25%)
  matrix products  14.6 us (8%)
  between operations  13.5 us (8%)
  local copies, waits for them, and re-layouts  10.2 us (6%)
  starting transfers between devices  8.15 us (5%)
    all_to_all x1, blocking collectives, from_everyone(): lax.all_to_all(jnp.broadcast_to(shard[None], (size, *shard.shape)), axis,...  29.6 us
    all_gather x1, waiting for transfers between devices, clique_filter(): lax.all_gather(blocks, 'row', axis=0, tiled=True)  28.2 us
    all_gather x1, waiting for transfers between devices, clique_filter(): lax.all_gather(mixer_blocks, 'row', axis=0, tiled=True)  23.5 us
    all_to_all x1, waiting for transfers between devices, from_everyone(): lax.all_to_all(jnp.broadcast_to(shard[None], (size, *shard.shape)), axis,...  23.1 us
    dot_general x2, matrix products, fold_with(): jnp.einsum('htab,tgbc->hgac', panel, piece, preferred_element_type=jnp.fl...  14.6 us
    all_to_all x1, blocking collectives, clique_filter(): lax.all_to_all(ordered, 'inner', split_axis=0, concat_axis=2, tiled=True)  13.4 us
    all_to_all x1, waiting for transfers between devices, clique_filter(): lax.all_to_all(filtered[None], 'inner', split_axis=2, concat_axis=0, tile...  8.25 us
    all_to_all x1, starting transfers between devices, from_everyone(): lax.all_to_all(jnp.broadcast_to(shard[None], (size, *shard.shape)), axis,...  4.14 us
  transfers between devices with their start and end apart: 4, of which 4 were waited for; matrix products, arithmetic and copies ran while one was open for 3% of the time, Pallas kernels for 0%

commit v1 on v0

--- a/solution.py
+++ b/solution.py
@@ -40,9 +40,12 @@
     slot_count = blocks.shape[1]
     slot_start = lax.axis_index("col") * slot_count
     density_panel = gathered_copies(blocks, "col", 1)
-    square = fold_with(density_panel, lax.all_gather(blocks, "row", axis=0, tiled=True)).astype(
-        jnp.bfloat16
-    )
+    square = fold_with(
+        density_panel,
+        jnp.concatenate(
+            lax.all_to_all(jnp.stack([blocks] * lax.axis_size("row")), "row", 0, 0), axis=0
+        ),
+    ).astype(jnp.bfloat16)
     group_ids = first_group + jnp.arange(groups_here, dtype=jnp.int32)
     slot_ids = slot_start + jnp.arange(slot_count, dtype=jnp.int32)
     on_diagonal = (group_ids[:, None] == slot_ids[None, :]).astype(jnp.float32)

time: 175 us -> 340 us (1.94)
  waiting for transfers between devices: 83 us -> 213 us
  blocking collectives: 43.1 us -> 69.2 us
  starting transfers between devices: 8.15 us -> 15.9 us
    all_to_all x1, waiting for transfers between devices: 23.1 us -> 182 us  [clique_filter(): lax.all_to_all(jnp.stack([blocks] * lax.axis_size('row')), 'row', 0, 0)]
    all_gather x1 -> x0, waiting for transfers between devices: 28.2 us -> none  [clique_filter(): lax.all_gather(blocks, 'row', axis=0, tiled=True)]
    all_to_all x1 -> x2, blocking collectives: 29.6 us -> 55.8 us  [from_everyone(): lax.all_to_all(jnp.broadcast_to(shard[None], (size, *shard.shape)), axis,...]
    all_to_all x1, starting transfers between devices: 4.14 us -> 11.8 us  [clique_filter(): lax.all_to_all(jnp.stack([blocks] * lax.axis_size('row')), 'row', 0, 0)]
    another operation x0 -> x1, local copies, waits for them, and re-layouts: none -> 4.26 us  [clique_filter(): jnp.stack([blocks] * lax.axis_size('row'))]
  transfers between devices with their start and end apart: 4 -> 3, of which waited for: 4 -> 3; matrix products, arithmetic and copies ran while one was open for 3% -> 1% of each run, Pallas kernels for 0% -> 0%
where the time goes in v1:
time: 340 us
  waiting for transfers between devices  213 us (63%)
  blocking collectives  69.2 us (20%)
  starting transfers between devices  15.9 us (5%)
  matrix products  14.5 us (4%)
  between operations  13.5 us (4%)
  local copies, waits for them, and re-layouts  12.2 us (4%)
    all_to_all x1, waiting for transfers between devices, clique_filter(): lax.all_to_all(jnp.stack([blocks] * lax.axis_size('row')), 'row', 0, 0)  182 us
    all_to_all x2, blocking collectives, from_everyone(): lax.all_to_all(jnp.broadcast_to(shard[None], (size, *shard.shape)), axis,...  55.8 us
    all_gather x1, waiting for transfers between devices, clique_filter(): lax.all_gather(mixer_blocks, 'row', axis=0, tiled=True)  22.6 us
    dot_general x2, matrix products, fold_with(): jnp.einsum('htab,tgbc->hgac', panel, piece, preferred_element_type=jnp.fl...  14.5 us
    all_to_all x1, blocking collectives, clique_filter(): lax.all_to_all(ordered, 'inner', split_axis=0, concat_axis=2, tiled=True)  13.4 us
    all_to_all x1, starting transfers between devices, clique_filter(): lax.all_to_all(jnp.stack([blocks] * lax.axis_size('row')), 'row', 0, 0)  11.8 us
    all_to_all x1, waiting for transfers between devices, clique_filter(): lax.all_to_all(filtered[None], 'inner', split_axis=2, concat_axis=0, tile...  8.25 us
  transfers between devices with their start and end apart: 3, of which 3 were waited for; matrix products, arithmetic and copies ran while one was open for 1% of the time, Pallas kernels for 0%

profile of v1, /device:TPU:1, one launch (start us, length us, event | category | flops | bytes accessed | tf_op | source)
XLA Modules:
  0.0 339.6 jit_solution(7860372055999071410)
XLA Ops:
  6.5 0.0 copy-start
  6.5 0.8 fusion.14
  7.3 0.3 copy-done
  7.6 0.6 gather_fusion
  8.2 0.2 copy.13
  8.4 13.4 %all_to_all.36 = bf16[4,1,1,256,256]{3,4,2,1,0:T(8,128)(2,1)S(1)} all-to-all(bf16[4,1,1,256,256]{3,4,2,1,0:T(8,128)(2,1)S(1)} %copy.13), channel_id=1, replica_groups=mesh['row'=16,'col'=4,'inner'=4] {'inner'}, dimensions={0} | all-to-all | bytes 1048576 | tf_op jit(solution)/shard_map/all_to_all | solution.py:38
  21.8 0.2 copy.16
  22.0 0.2 broadcast_in_dim.8
  22.2 27.9 %all_to_all.37 = bf16[4,1,4,256,256]{4,3,2,1,0:T(8,128)(2,1)S(1)} all-to-all(bf16[4,1,4,256,256]{4,3,2,1,0:T(8,128)(2,1)S(1)} %broadcast_in_dim.8), channel_id=1, replica_groups=mesh['row'=16,'col'=4,'inner'=4] {'col'}, dimensions={0} | all-to-all | bytes 4194304 | tf_op jit(solution)/shard_map/all_to_all | solution.py:17
  50.1 4.3 %stack.3 = bf16[16,1,4,256,256]{3,4,2,1,0:T(8,128)(2,1)} broadcast(bf16[4,256,256]{1,2,0:T(8,128)(2,1)S(1)} %bitcast.68), dimensions={2,3,4} | broadcast | bytes 8912896 | tf_op jit(solution)/shard_map/stack | solution.py:46
  54.3 0.0 copy-start.1
  54.3 11.8 %all-to-all-start.1 = ((bf16[16,1,4,256,256]{3,4,2,1,0:T(8,128)(2,1)}), bf16[16,1,4,256,256]{3,4,2,1,0:T(8,128)(2,1)}, u32[]{:S(2)}, u32[]{:S(2)}) async-start(bf16[16,1,4,256,256]{3,4,2,1,0:T(8,128)(2,1)} %stack.3), calls=%async_computation.1 | async-start | bytes 16777216 | tf_op jit(solution)/shard_map/all_to_all | solution.py:46
  66.2 0.0 all-gather.2.cloned.1.call-start
  66.2 0.0 copy-done.1
  66.3 0.6 fusion.16
  66.9 0.6 compare_select_fusion.2
  67.6 182.0 %all-to-all-done.1 = bf16[16,1,4,256,256]{3,4,2,1,0:T(8,128)(2,1)} async-done(((bf16[16,1,4,256,256]{3,4,2,1,0:T(8,128)(2,1)}), bf16[16,1,4,256,256]{3,4,2,1,0:T(8,128)(2,1)}, u32[]{:S(2)}, u32[]{:S(2)}) %all-to-all-start.1) | async-done | bytes 8388640 | tf_op jit(solution)/shard_map/all_to_all | solution.py:46
  249.6 8.0 %fusion.12 = (bf16[1,4,256,256]{2,3,1,0:T(8,128)(2,1)}, bf16[4,256,256]{2,1,0:T(8,128)(2,1)}) fusion(bf16[4,1,1,256,256]{3,4,2,1,0:T(8,128)(2,1)S(1)} %all_to_all.36, f32[]{:T(128)} %bitcast.7, f32[]{:T(128)} %bitcast.1, f32[256,256]{0,1:T(8,128)S(1)} %fusion.13, f32[4]{0:T(128)S(1)} %compare_select_fusion.2, bf16[16,256,256,1]{2,1,0,3:T(8,128)(2,1)S(1)} %bitcast.69, ...), kind=kOutput, calls=%fused_computation.12 | convolution fusion | flops 2149842944 | bytes 12320792 | tf_op jit(solution)/shard_map/htab,tgbc->hgac/dot_general | solution.py:27
  257.6 2.1 copy.17
  259.7 0.0 all-gather.2.cloned.1.call-update
  259.7 1.2 copy.18
  260.9 0.2 broadcast_in_dim.10
  261.1 27.9 %all_to_all.38 = bf16[4,1,4,256,256]{4,3,2,1,0:T(8,128)(2,1)S(1)} all-to-all(bf16[4,1,4,256,256]{4,3,2,1,0:T(8,128)(2,1)S(1)} %broadcast_in_dim.10), channel_id=1, replica_groups=mesh['row'=16,'col'=4,'inner'=4] {'col'}, dimensions={0} | all-to-all | bytes 4194304 | tf_op jit(solution)/shard_map/all_to_all | solution.py:17
  289.1 22.6 %all-gather.2.cloned.1.call-done = bf16[16,4,256,256]{3,2,1,0:T(8,128)(2,1)} async-done(((bf16[1,4,256,256]{3,2,1,0:T(8,128)(2,1)}), bf16[16,4,256,256]{3,2,1,0:T(8,128)(2,1)}) %all-gather.2.cloned.1.call-update) | async-done | bytes 8388624 | tf_op jit(solution)/shard_map/all_gather | solution.py:60
  311.6 6.6 %fusion.10 = bf16[1,1,4,256,256]{3,4,1,0,2:T(8,128)(2,1)} fusion(bf16[16,4,256,256]{3,2,1,0:T(8,128)(2,1)} %all-gather.2.cloned.1.call-done, bf16[16,256,256,1]{2,1,3,0:T(8,128)(2,1)S(1)} %bitcast.70), kind=kOutput, calls=%fused_computation.9 | convolution fusion | flops 2147745792 | bytes 11010048 | tf_op jit(solution)/shard_map/htab,tgbc->hgac/dot_general | solution.py:27
  318.2 4.0 %all-to-all-start.4 = ((bf16[1,1,4,256,256]{3,4,1,0,2:T(8,128)(2,1)}), bf16[1,1,4,256,256]{3,4,1,0,2:T(8,128)(2,1)S(1)}, u32[]{:S(2)}, u32[]{:S(2)}) async-start(bf16[1,1,4,256,256]{3,4,1,0,2:T(8,128)(2,1)} %fusion.10), calls=%async_computation.4 | async-start | bytes 1048576 | tf_op jit(solution)/shard_map/all_to_all | solution.py:62
  322.2 0.7 slice.19
  322.9 0.1 fusion.15
  322.9 8.2 %all-to-all-done.4 = bf16[1,1,4,256,256]{3,4,1,0,2:T(8,128)(2,1)S(1)} async-done(((bf16[1,1,4,256,256]{3,4,1,0,2:T(8,128)(2,1)}), bf16[1,1,4,256,256]{3,4,1,0,2:T(8,128)(2,1)S(1)}, u32[]{:S(2)}, u32[]{:S(2)}) %all-to-all-start.4) | async-done | bytes 524320 | tf_op jit(solution)/shard_map/all_to_all | solution.py:62
  331.2 0.6 gather_fusion.1
  331.8 1.0 copy.21
  (3 shorter events, 0.0 us)
Async XLA Ops:
  6.5 1.1 copy-start
  54.3 11.9 %copy-start.1 = (f32[3]{0:T(128)S(1)}, f32[3]{0:T(128)}, u32[]{:S(2)}) copy-start(f32[3]{0:T(128)} %param.5) | copy-start | bytes 40
  54.3 195.2 %all-to-all-start.1 = ((bf16[16,1,4,256,256]{3,4,2,1,0:T(8,128)(2,1)}), bf16[16,1,4,256,256]{3,4,2,1,0:T(8,128)(2,1)}, u32[]{:S(2)}, u32[]{:S(2)}) async-start(bf16[16,1,4,256,256]{3,4,2,1,0:T(8,128)(2,1)} %stack.3), calls=%async_computation.1 | async-start | bytes 16777216 | tf_op jit(solution)/shard_map/all_to_all | solution.py:46
  66.2 245.4 %all-gather.2.cloned.1.call-start = ((), (), s32[]{:S(2)}) async-start(), calls=%async_computation.5 | async-start | bytes 8912896 | tf_op jit(solution)/shard_map/all_gather | solution.py:60
  318.2 13.0 %all-to-all-start.4 = ((bf16[1,1,4,256,256]{3,4,1,0,2:T(8,128)(2,1)}), bf16[1,1,4,256,256]{3,4,1,0,2:T(8,128)(2,1)S(1)}, u32[]{:S(2)}, u32[]{:S(2)}) async-start(bf16[1,1,4,256,256]{3,4,1,0,2:T(8,128)(2,1)} %fusion.10), calls=%async_computation.4 | async-start | bytes 1048576 | tf_op jit(solution)/shard_map/all_to_all | solution.py:62
Sparse Core Ops, SparseCore 0:
  259.8 51.7 all-gather.1
